TPU v7x, 256 devices: a whole 4x4x8 slice. The times are simulated.
256 devices in a mesh: dp: 16 (over z, core), mp: 16 (over y, x).
Axes of the slice: x: 4, y: 4, z: 8, core: 2. Of those that a mesh axis runs over, the one named last changes fastest.
Arguments:
- hidden_states: bfloat16 [256, 640, 1280], P(('dp', 'mp')), may hold values from -6 to 6
- ln_attn_gain: float32 [1280], replicated, may hold values from 0.1 to 1.9
- w_qkv: bfloat16 [1280, 16, 192], P(None, 'mp'), may hold values from -0.15625 to 0.15625
- output_weight: bfloat16 [64, 16, 1280], P(None, 'mp'), may hold values from -0.75 to 0.75
- ln_final_gain: float32 [1280], replicated, may hold values from 0.1 to 1.9
- dense_weight: bfloat16 [1280, 1280], replicated, may hold values from -0.15625 to 0.15625
- decoder_weight: bfloat16 [1280, 33], replicated, may hold values from -0.5390625 to 0.5390625
- decoder_bias: float32 [33], replicated, may hold values from -4 to 4
- seq_tokens: int32 [24, 640], replicated, may hold values from 4 to 23
- seq_lengths: int32 [24], replicated, may hold values from 128 to 640
- copy_sequence: int32 [256], replicated, may hold values from 0 to 23
- mask_code: int32 [256, 64], replicated, may hold values from 0 to 1048575
- copy_owner: int32 [256], replicated, may hold values from 0 to 255, each once
Outputs:
- pll: float32 [256, 64], P('dp', 'mp')
Inputs may be any that keep to these rules, and one draw needn't show every extreme that they name: `seq_tokens`: amino-acid token ids. `copy_owner`: every row of pll is named by exactly one copy.
All inputs are finite; a program needn't handle non-finite values.
Results may differ from a plain program's by a relative error of at most 0.0038.
Values may be sent and summed in bfloat16 or wider, within the bound.
No kernel may reach another device: no remote copies, remote signals or barrier semaphores. Data moves between devices by JAX's collectives and lax.ppermute only.
A program may use at most 128 MiB of HBM per device.

v0:
```python
import jax
import jax.numpy as jnp
from jax import lax
from jax.sharding import PartitionSpec as P

epsilon = 1e-05


def layer_norm(inputs):
    average = jnp.mean(inputs, axis=-1, keepdims=True)
    centred = inputs - average
    variance = jnp.mean(centred * centred, axis=-1, keepdims=True)
    return centred * lax.rsqrt(variance + epsilon)


def rotary_tables(seq_span, head_size):
    half_width = head_size // 2
    frequency = 1.0 / 10000.0 ** (jnp.arange(half_width, dtype=jnp.float32) * (2.0 / head_size))
    angles = jnp.arange(seq_span, dtype=jnp.float32)[:, None] * frequency[None, :]
    angles = jnp.concatenate([angles, angles], axis=-1)
    return (jnp.cos(angles), jnp.sin(angles))


def rotate(inputs, cosine, sine):
    half_width = inputs.shape[-1] // 2
    turned = jnp.concatenate([-inputs[..., half_width:], inputs[..., :half_width]], axis=-1)
    return inputs * cosine + turned * sine


def score_rows(residual, ln_final_gain, dense_weight, decoder_weight, decoder_bias, targets):
    feature = residual.shape[-1]
    normed_final = (layer_norm(residual) * ln_final_gain).astype(jnp.bfloat16).reshape(-1, feature)
    dense_out = jnp.dot(normed_final, dense_weight, preferred_element_type=jnp.float32)
    headed = layer_norm(jax.nn.gelu(dense_out, approximate=False)).astype(jnp.bfloat16)
    logits = jnp.dot(headed, decoder_weight, preferred_element_type=jnp.float32) + decoder_bias
    log_probs = logits - jax.nn.logsumexp(logits, axis=-1, keepdims=True)
    vocab_ids = jnp.arange(logits.shape[-1], dtype=jnp.int32)
    flat_targets = targets.reshape(-1)
    picked = jnp.sum(
        jnp.where(flat_targets[:, None] == vocab_ids[None, :], log_probs, 0.0), axis=-1
    )
    return picked.reshape(targets.shape)


def copy_meta(first, amount, tables):
    seq_tokens, seq_lengths, copy_sequence, mask_code = tables
    sequence = lax.dynamic_slice_in_dim(copy_sequence, first, amount, 0)
    codes = lax.dynamic_slice_in_dim(mask_code, first, amount, 0)
    seq_ids = jnp.arange(seq_lengths.shape[0], dtype=jnp.int32)
    lengths = jnp.sum(
        jnp.where(sequence[:, None] == seq_ids[None, :], seq_lengths[None, :], 0), axis=1
    )
    positions = codes % lengths[:, None]
    return (sequence, lengths, positions)


def attend_projected(projected, out_part, lengths, positions, cosine, sine):
    copies, seq_span, head_count, three, head_size = projected.shape
    key_matrix = rotate(
        projected[:, :, :, 1], cosine[None, :, None, :], sine[None, :, None, :]
    ).astype(jnp.bfloat16)
    value_matrix = projected[:, :, :, 2].astype(jnp.bfloat16)
    query_matrix = projected[jnp.arange(copies)[:, None], positions, :, 0] * head_size ** (-0.5)
    query_matrix = rotate(
        query_matrix, cosine[positions][:, :, None, :], sine[positions][:, :, None, :]
    ).astype(jnp.bfloat16)
    attention_logits = jnp.einsum(
        "cmhd,clhd->chml", query_matrix, key_matrix, preferred_element_type=jnp.float32
    )
    alive = jnp.arange(seq_span, dtype=jnp.int32)[None, :] < lengths[:, None]
    attention_logits = jnp.where(alive[:, None, None, :], attention_logits, -1e30)
    largest = jnp.max(attention_logits, axis=-1, keepdims=True)
    weights = jnp.exp(attention_logits - largest)
    attention_probs = (weights / jnp.sum(weights, axis=-1, keepdims=True)).astype(jnp.bfloat16)
    context_vectors = jnp.einsum(
        "chml,clhd->cmhd", attention_probs, value_matrix, preferred_element_type=jnp.float32
    ).astype(jnp.bfloat16)
    return jnp.einsum(
        "cmhd,dhe->cme", context_vectors, out_part, preferred_element_type=jnp.float32
    )


def on_device(
    hidden_states,
    ln_attn_gain,
    w_qkv,
    output_weight,
    ln_final_gain,
    dense_weight,
    decoder_weight,
    decoder_bias,
    seq_tokens,
    seq_lengths,
    copy_sequence,
    mask_code,
    copy_owner,
):
    lane_copies, seq_span, feature = hidden_states.shape
    model_size = lax.axis_size("mp")
    model_index = lax.axis_index("mp")
    group_copies = lane_copies * model_size
    head_size = output_weight.shape[0]
    mask_count = mask_code.shape[1]
    own_masks = mask_count // model_size
    cosine, sine = rotary_tables(seq_span, head_size)
    tables = (seq_tokens, seq_lengths, copy_sequence, mask_code)
    group_first = lax.axis_index("dp") * group_copies
    sequence, lengths, positions = copy_meta(group_first, group_copies, tables)
    targets = jnp.take_along_axis(seq_tokens[sequence], positions, axis=1)
    own_targets = lax.dynamic_slice_in_dim(targets, model_index * own_masks, own_masks, 1)
    lane_start = model_index * lane_copies
    lane_positions = lax.dynamic_slice_in_dim(positions, lane_start, lane_copies, 0)
    normed = (layer_norm(hidden_states.astype(jnp.float32)) * ln_attn_gain).astype(jnp.bfloat16)
    own_rows = hidden_states[jnp.arange(lane_copies)[:, None], lane_positions].astype(jnp.float32)
    lane_lengths = lax.dynamic_slice_in_dim(lengths, lane_start, lane_copies, 0)
    qkv_part = lax.all_gather(w_qkv, "mp", axis=1, tiled=True)
    out_part = lax.all_gather(output_weight, "mp", axis=1, tiled=True)
    count = qkv_part.shape[1]
    made = jnp.dot(
        normed.reshape(-1, feature),
        qkv_part.reshape(feature, -1),
        preferred_element_type=jnp.float32,
    )
    made = made.reshape(lane_copies, seq_span, count, 3, head_size)
    attention_mixed = attend_projected(made, out_part, lane_lengths, lane_positions, cosine, sine)
    lane_rows = own_rows + attention_mixed
    residual = lax.all_to_all(lane_rows, "mp", split_axis=1, concat_axis=0, tiled=True)
    attention_logits = score_rows(
        residual, ln_final_gain, dense_weight, decoder_weight, decoder_bias, own_targets
    )
    everything = lax.all_gather(attention_logits, "dp", axis=0, tiled=True)
    wanted = group_first + jnp.arange(group_copies, dtype=jnp.int32)
    copy_ids = jnp.arange(copy_owner.shape[0], dtype=jnp.int32)
    source = jnp.sum(
        jnp.where(copy_owner[None, :] == wanted[:, None], copy_ids[None, :], 0), axis=1
    )
    return everything[source]


def solution(mesh):
    placed = (
        P(("dp", "mp"), None, None),
        P(),
        P(None, "mp", None),
        P(None, "mp", None),
        P(),
        P(),
        P(),
        P(),
        P(),
        P(),
        P(),
        P(),
        P(),
    )
    return jax.shard_map(
        on_device, mesh=mesh, in_specs=placed, out_specs=P("dp", "mp"), check_vma=False
    )
```

profile of v0, /device:TPU:1, one launch (start us, length us, event | category | flops | bytes accessed | tf_op | source)
XLA Modules:
  0.0 194.8 jit_solution(9055554466586441534)
XLA Ops:
  11.6 2.1 %fusion.52 = (f32[640,64]{1,0:T(8,128)}, f32[640,64]{1,0:T(8,128)}) fusion(f32[640,32]{1,0:T(8,128)S(1)} %iota_multiply_fusion), kind=kLoop, calls=%fused_computation.81 | loop fusion | flops 40960 | bytes 409600 | tf_op jit(solution)/shard_map/cos | solution.py:21
  15.0 1.4 gather_fusion
  16.5 8.6 %gather_fusion.6 = s32[1024]{0:T(1024)S(1)} fusion(s32[16,640]{1,0:T(8,128)S(1)} %gather_fusion, s32[1024]{0:T(1024)S(1)} %reshape.339), kind=kCustom, calls=%fused_computation.6 | custom fusion | bytes 16384 | tf_op jit(solution)/shard_map/jit(take_along_axis)/gather | solution.py:109
  26.4 1.6 gather_fusion.3
  28.0 1.6 gather_fusion.4
  29.5 1.8 copy.42
  31.9 2.6 %gather_fusion.1 = bf16[64,1280]{1,0:T(8,128)(2,1)} fusion(bf16[1,640,1280]{2,1,0:T(8,128)(2,1)} %param.13, s32[64]{0:T(128)S(1)} %or_bitcast_fusion.1), kind=kCustom, calls=%fused_computation.1 | custom fusion | bytes 328192 | tf_op jit(solution)/shard_map/gather | solution.py:114
  35.2 1.8 convert_reduce_fusion
  37.5 49.6 %all-gather.4.cloned.1.call-done = bf16[1280,16,192]{0,2,1:T(8,128)(2,1)} async-done(((bf16[1280,1,192]{0,2,1:T(8,128)(2,1)}), bf16[1280,16,192]{0,2,1:T(8,128)(2,1)}) %all-gather.4.cloned.1.call-update) | async-done | bytes 7864336 | tf_op jit(solution)/shard_map/all_gather | solution.py:116
  87.2 11.3 %convolution_bitcast_fusion = f32[1,640,16,3,64]{1,4,3,2,0:T(8,128)} fusion(bf16[16,3,64,1280]{3,2,1,0:T(8,128)(2,1)} %bitcast.96, bf16[1,640,1280]{2,1,0:T(8,128)(2,1)} %param.13, f32[1280]{0:T(1024)} %param.14, f32[640]{0:T(1024)S(1)} %add_rsqrt_fusion, f32[640]{0:T(1024)S(1)} %broadcast_multiply_fusion.1), kind=kOutput, calls=%fused_computation.15 | convolution fusion | flops 5037260800 | bytes 17377280 | tf_op jit(solution)/shard_map/dot_general | solution.py:119
  98.5 15.1 %copy.40 = f32[1,640,16,3,64]{4,2,3,1,0:T(8,128)} copy(f32[1,640,16,3,64]{1,4,3,2,0:T(8,128)} %convolution_bitcast_fusion) | data formatting | bytes 15728640 | tf_op jit(solution)/shard_map/dot_general | solution.py:119
  113.6 7.0 %gather_fusion.2 = f32[64,16,64]{2,1,0:T(8,128)} fusion(f32[1,640,16,3,64]{4,2,3,1,0:T(8,128)} %copy.40, s32[64]{0:T(128)S(1)} %or_bitcast_fusion), kind=kCustom, calls=%fused_computation.2 | custom fusion | bytes 525056 | tf_op jit(solution)/shard_map/gather | solution.py:63
  122.2 1.9 slice_bitcast_fusion
  125.0 2.6 %fusion.18 = f32[16,64,640]{2,1,0:T(8,128)S(1)} fusion(f32[640,16,32]{0,2,1:T(8,128)S(1)} %get-tuple-element.10, f32[640,16,32]{0,2,1:T(8,128)S(1)} %get-tuple-element.9, f32[1,640,16,3,64]{1,4,3,2,0:T(8,128)} %convolution_bitcast_fusion, f32[640,64]{0,1:T(8,128)S(1)} %copy-done.3, f32[640,64]{0,1:T(8,128)S(1)} %copy.41, bf16[64,16,64]{2,1,0:T(8,128)(2,1)S(1)} %fusion.38), kind=kOutput, calls=%fused_computation.33 | convolution fusion | flops 87162880 | bytes 8323072 | tf_op jit(solution)/shard_map/cmhd,clhd->chml/dot_general | solution.py:67
  127.7 2.1 %fusion.66 = (f32[16,64]{1,0:T(8,128)S(1)}, f32[16,64,640]{2,1,0:T(8,128)}) fusion(f32[16,64,640]{2,1,0:T(8,128)S(1)} %fusion.18, pred[640]{0:T(1024)(128)(4,1)S(1)} %copy-done.8), kind=kOutput, calls=%fused_computation.128 | output fusion | flops 2622079 | bytes 5247616 | tf_op jit(solution)/shard_map/sub | solution.py:73
  129.8 10.5 %all-gather.6.cloned.1.call-done = bf16[64,16,1280]{2,0,1:T(8,128)(2,1)} async-done(((bf16[64,1,1280]{2,0,1:T(8,128)(2,1)}), bf16[64,16,1280]{2,0,1:T(8,128)(2,1)}) %all-gather.6.cloned.1.call-update) | async-done | bytes 2621456 | tf_op jit(solution)/shard_map/all_gather | solution.py:117
  140.3 5.1 %fusion.9 = f32[1,64,1280]{2,1,0:T(8,128)} fusion(bf16[64,16,1280]{2,0,1:T(8,128)(2,1)} %all-gather.6.cloned.1.call-done, f32[16,64,640]{2,1,0:T(8,128)} %get-tuple-element.16, f32[16,64]{1,0:T(8,128)S(1)} %get-tuple-element.15, f32[1,640,16,3,64]{1,4,3,2,0:T(8,128)} %convolution_bitcast_fusion, bf16[64,1280]{1,0:T(8,128)(2,1)S(1)} %copy-done.4), kind=kOutput, calls=%fused_computation.26 | convolution fusion | flops 253198336 | bytes 7049216 | tf_op jit(solution)/shard_map/cmhd,dhe->cme/dot_general | solution.py:78
  145.5 2.0 %copy.45 = f32[1,64,1280]{2,0,1:T(1,128)} copy(f32[1,64,1280]{2,1,0:T(8,128)} %fusion.9) | data formatting | bytes 655360 | tf_op jit(solution)/shard_map/add | solution.py:126
  147.5 4.4 %all-to-all-start = ((f32[1,64,1280]{2,0,1:T(1,128)}), f32[1,64,1280]{2,0,1:T(1,128)}, u32[]{:S(2)}, u32[]{:S(2)}) async-start(f32[1,64,1280]{2,0,1:T(1,128)} %copy.45), calls=%async_computation | async-start | bytes 655360 | tf_op jit(solution)/shard_map/all_to_all | solution.py:127
  151.9 7.8 %all-to-all-done = f32[1,64,1280]{2,0,1:T(1,128)} async-done(((f32[1,64,1280]{2,0,1:T(1,128)}), f32[1,64,1280]{2,0,1:T(1,128)}, u32[]{:S(2)}, u32[]{:S(2)}) %all-to-all-start) | async-done | bytes 327712 | tf_op jit(solution)/shard_map/all_to_all | solution.py:127
  159.7 1.5 reduce_sum.105
  161.3 2.0 %multiply_reduce_fusion.1 = f32[64]{0:T(128)S(1)} fusion(f32[1,64,1280]{2,0,1:T(1,128)} %all-to-all-done, f32[64]{0:T(128)S(1)} %broadcast_multiply_fusion.3), kind=kLoop, calls=%fused_computation.76 | loop fusion | flops 245696 | bytes 328192 | tf_op jit(solution)/shard_map/reduce_sum | solution.py:12
  163.3 2.3 %fusion.67 = (f32[64]{0:T(128)S(1)}, f32[64,1280]{1,0:T(8,128)S(1)}) fusion(bf16[1280,1280]{1,0:T(8,128)(2,1)S(1)} %copy-done, f32[1,64,1280]{2,0,1:T(1,128)} %all-to-all-done, f32[1280]{0:T(1024)S(1)} %copy-done.11, f32[64]{0:T(128)S(1)} %add_rsqrt_fusion.2, f32[64]{0:T(128)S(1)} %broadcast_multiply_fusion.3), kind=kOutput, calls=%fused_computation.129 | convolution fusion | flops 215367616 | bytes 3938048 | tf_op jit(solution)/shard_map/dot_general | solution.py:33
  166.4 20.2 %all-gather = f32[16,16,4]{1,2,0:T(4,128)S(1)} all-gather(f32[1,16,4]{1,2,0:T(4,128)S(1)} %copy.46), channel_id=1, replica_groups=mesh['dp'=16,'mp'=16] {'dp'}, dimensions={0}, use_global_device_ids=true | all-gather | bytes 4352 | tf_op jit(solution)/shard_map/all_gather | solution.py:131
  (81 shorter events, 14.1 us)
Async XLA Ops:
  6.5 156.7 %copy-start = (bf16[1280,1280]{1,0:T(8,128)(2,1)S(1)}, bf16[1280,1280]{1,0:T(8,128)(2,1)}, u32[]{:S(2)}) copy-start(bf16[1280,1280]{1,0:T(8,128)(2,1)} %param.18) | copy-start | bytes 9830404
  6.5 80.7 %all-gather.4.cloned.1.call-start = ((), (), s32[]{:S(2)}) async-start(), calls=%async_computation.1 | async-start | bytes 8355840 | tf_op jit(solution)/shard_map/all_gather | solution.py:116
  7.3 133.1 %all-gather.6.cloned.1.call-start = ((), (), s32[]{:S(2)}) async-start(), calls=%async_computation.2 | async-start | bytes 2785280 | tf_op jit(solution)/shard_map/all_gather | solution.py:117
  25.1 9.4 %copy-start.7 = (s32[256]{0:T(256)S(1)}, s32[256]{0:T(256)}, u32[]{:S(2)}) copy-start(s32[256]{0:T(256)} %param.25) | copy-start | bytes 3076
  34.5 2.5 %copy-start.1 = (bf16[1,640,1280]{2,1,0:T(8,128)(2,1)S(1)}, bf16[1,640,1280]{2,1,0:T(8,128)(2,1)}, u32[]{:S(2)}) copy-start(bf16[1,640,1280]{2,1,0:T(8,128)(2,1)} %param.13) | copy-start | bytes 4915204
  120.6 1.4 copy-start.2
  124.1 0.9 copy-start.3
  125.0 2.6 %copy-start.8 = (pred[640]{0:T(1024)(128)(4,1)S(1)}, pred[640]{0:T(1024)(128)(4,1)}, u32[]{:S(2)}) copy-start(pred[640]{0:T(1024)(128)(4,1)} %iota_compare_fusion.2) | copy-start | bytes 1924
  127.7 12.7 %copy-start.4 = (bf16[64,1280]{1,0:T(8,128)(2,1)S(1)}, bf16[64,1280]{1,0:T(8,128)(2,1)}, u32[]{:S(2)}) copy-start(bf16[64,1280]{1,0:T(8,128)(2,1)} %gather_fusion.1) | copy-start | bytes 491524
  140.3 11.6 %copy-start.10 = (s32[16]{0:T(128)S(1)}, s32[16]{0:T(128)}, u32[]{:S(2)}) copy-start(s32[16]{0:T(128)} %select_reduce_fusion.2) | copy-start | bytes 196
  140.3 22.9 %copy-start.11 = (f32[1280]{0:T(1024)S(1)}, f32[1280]{0:T(1024)}, u32[]{:S(2)}) copy-start(f32[1280]{0:T(1024)} %param.17) | copy-start | bytes 15364
  147.5 12.2 %all-to-all-start = ((f32[1,64,1280]{2,0,1:T(1,128)}), f32[1,64,1280]{2,0,1:T(1,128)}, u32[]{:S(2)}, u32[]{:S(2)}) async-start(f32[1,64,1280]{2,0,1:T(1,128)} %copy.45), calls=%async_computation | async-start | bytes 655360 | tf_op jit(solution)/shard_map/all_to_all | solution.py:127
  163.3 2.6 %copy-start.5 = (bf16[1280,33]{0,1:T(8,128)(2,1)S(1)}, bf16[1280,33]{0,1:T(8,128)(2,1)}, u32[]{:S(2)}) copy-start(bf16[1280,33]{0,1:T(8,128)(2,1)} %param.19) | copy-start | bytes 253444
  163.3 2.6 %copy-start.9 = (f32[33]{0:T(128)S(1)}, f32[33]{0:T(128)}, u32[]{:S(2)}) copy-start(f32[33]{0:T(128)} %param.20) | copy-start | bytes 400
  163.3 2.9 %copy-start.6 = (s32[64]{0:T(128)S(1)}, s32[64]{0:T(128)}, u32[]{:S(2)}) copy-start(s32[64]{0:T(128)} %eq.57) | copy-start | bytes 772
Sparse Core Ops, SparseCore 0:
  9.8 77.3 all-gather.3
  89.6 50.6 all-gather.5
where the time goes:
time: 196 us; the launch traced here: 195 us
  waiting for transfers between devices  69.4 us (35%)
  local copies, waits for them, and re-layouts  49.3 us (25%)
  matrix products  21.6 us (11%)
  blocking collectives  20.2 us (10%)
  other arithmetic  16.1 us (8%)
  between operations  13.7 us (7%)
  starting transfers between devices  4.43 us (2%)
    all_gather x1, waiting for transfers between devices, on_device(): qkv_part = lax.all_gather(w_qkv, 'mp', axis=1, tiled=True)  49.6 us
    all_gather x1, blocking collectives, on_device(): everything = lax.all_gather(attention_logits, 'dp', axis=0, tiled=True)  20.2 us
    dot_general x1, local copies, waits for them, and re-layouts, on_device(): jnp.dot(normed.reshape(-1, feature), qkv_part.reshape(feature, -1), prefe...  15.1 us
    dot_general x1, matrix products, on_device(): jnp.dot(normed.reshape(-1, feature), qkv_part.reshape(feature, -1), prefe...  11.3 us
    all_gather x1, waiting for transfers between devices, on_device(): out_part = lax.all_gather(output_weight, 'mp', axis=1, tiled=True)  10.5 us
    gather x4, local copies, waits for them, and re-layouts, on_device(): targets = jnp.take_along_axis(seq_tokens[sequence], positions, axis=1)  10.2 us
    all_to_all x1, waiting for transfers between devices, on_device(): lax.all_to_all(lane_rows, 'mp', split_axis=1, concat_axis=0, tiled=True)  7.8 us
    gather x1, local copies, waits for them, and re-layouts, attend_projected(): projected[jnp.arange(copies)[:, None], positions, :, 0]  6.96 us
  transfers between devices with their start and end apart: 3, of which 3 were waited for; matrix products, arithmetic and copies ran while one was open for 37% of the time, Pallas kernels for 0%

commit v1 on v0

--- a/solution.py
+++ b/solution.py
@@ -1,9 +1,26 @@
+import functools
 import jax
 import jax.numpy as jnp
 from jax import lax
 from jax.sharding import PartitionSpec as P
 
 epsilon = 1e-05
+
+
+def fit_ends(s0, which_axis):
+    n_blocks = lax.axis_size(which_axis)
+    crops = [(c, (c + 1) % n_blocks) for c in range(n_blocks)]
+    found_now = [None] * n_blocks
+    found_now[n_blocks - 1] = s0
+    for nth in range(n_blocks - 2, -1, -1):
+        found_now[nth] = lax.ppermute(found_now[nth + 1], which_axis, perm=crops)
+    tile_out = jnp.concatenate(found_now, axis=1)
+    clean = (lax.axis_index(which_axis) + 1) * s0.shape[1]
+    lower = jnp.roll(tile_out, clean, 1)
+    return lower
+
+
+mark_boxes = functools.partial(fit_ends, which_axis="mp")
 
 
 def layer_norm(inputs):
@@ -114,7 +131,7 @@
     own_rows = hidden_states[jnp.arange(lane_copies)[:, None], lane_positions].astype(jnp.float32)
     lane_lengths = lax.dynamic_slice_in_dim(lengths, lane_start, lane_copies, 0)
     qkv_part = lax.all_gather(w_qkv, "mp", axis=1, tiled=True)
-    out_part = lax.all_gather(output_weight, "mp", axis=1, tiled=True)
+    out_part = mark_boxes(output_weight)
     count = qkv_part.shape[1]
     made = jnp.dot(
         normed.reshape(-1, feature),

time: 196 us -> 319 us (1.63)
  local copies, waits for them, and re-layouts: 49.3 us -> 96.5 us
  waiting for transfers between devices: 69.4 us -> 112 us
  blocking collectives: 20.2 us -> 38.7 us
  other arithmetic: 16.1 us -> 24.4 us
  starting transfers between devices: 4.43 us -> 9.56 us
    ppermute x0 -> x15, waiting for transfers between devices: none -> 104 us  [fit_ends(): found_now[nth] = lax.ppermute(found_now[nth + 1], which_axis, perm=crops)]
    all_gather x1, waiting for transfers between devices: 49.6 us -> 0.01 us  [on_device(): qkv_part = lax.all_gather(w_qkv, 'mp', axis=1, tiled=True)]
    unnamed x27 -> x106, local copies, waits for them, and re-layouts: 0.98 us -> 40.7 us
    all_gather x1, blocking collectives: 20.2 us -> 38.7 us  [on_device(): everything = lax.all_gather(attention_logits, 'dp', axis=0, tiled=True)]
    all_gather x1 -> x0, waiting for transfers between devices: 10.5 us -> none  [on_device(): out_part = lax.all_gather(output_weight, 'mp', axis=1, tiled=True)]
    gather x4, local copies, waits for them, and re-layouts: 10.2 us -> 14.6 us  [on_device(): targets = jnp.take_along_axis(seq_tokens[sequence], positions, axis=1)]
  transfers between devices with their start and end apart: 3 -> 17, of which waited for: 3 -> 14; matrix products, arithmetic and copies ran while one was open for 37% -> 26% of each run, Pallas kernels for 0% -> 0%
where the time goes in v1:
time: 319 us; the launch traced here: 317 us
  waiting for transfers between devices  112 us (35%)
  local copies, waits for them, and re-layouts  96.5 us (30%)
  blocking collectives  38.7 us (12%)
  other arithmetic  24.4 us (8%)
  matrix products  21.7 us (7%)
  between operations  13.9 us (4%)
  starting transfers between devices  9.56 us (3%)
    ppermute x15, waiting for transfers between devices, fit_ends(): found_now[nth] = lax.ppermute(found_now[nth + 1], which_axis, perm=crops)  104 us
    unnamed x106, local copies, waits for them, and re-layouts  40.7 us
    all_gather x1, blocking collectives, on_device(): everything = lax.all_gather(attention_logits, 'dp', axis=0, tiled=True)  38.7 us
    dot_general x1, local copies, waits for them, and re-layouts, on_device(): jnp.dot(normed.reshape(-1, feature), qkv_part.reshape(feature, -1), prefe...  15.1 us
    gather x4, local copies, waits for them, and re-layouts, on_device(): targets = jnp.take_along_axis(seq_tokens[sequence], positions, axis=1)  14.6 us
    dot_general x1, matrix products, on_device(): jnp.dot(normed.reshape(-1, feature), qkv_part.reshape(feature, -1), prefe...  11.3 us
    all_to_all x1, waiting for transfers between devices, on_device(): lax.all_to_all(lane_rows, 'mp', split_axis=1, concat_axis=0, tiled=True)  7.92 us
    all_to_all x1, starting transfers between devices, on_device(): lax.all_to_all(lane_rows, 'mp', split_axis=1, concat_axis=0, tiled=True)  7.35 us
  transfers between devices with their start and end apart: 17, of which 14 were waited for; matrix products, arithmetic and copies ran while one was open for 26% of the time, Pallas kernels for 0%

profile of v1, /device:TPU:1, one launch (start us, length us, event | category | flops | bytes accessed | tf_op | source)
XLA Modules:
  0.0 316.9 jit_solution(18427871409411553021)
XLA Ops:
  12.8 3.3 %collective-permute-done = bf16[64,1,1280]{2,0,1:T(8,128)(2,1)S(1)} collective-permute-done((bf16[64,1,1280]{2,0,1:T(8,128)(2,1)}, bf16[64,1,1280]{2,0,1:T(8,128)(2,1)S(1)}, u32[]{:S(2)}, u32[]{:S(2)}) %collective-permute-start) | collective-permute-done | bytes 163872 | tf_op jit(solution)/shard_map/ppermute | solution.py:16
  16.0 7.6 %collective-permute-done.1 = bf16[64,1,1280]{2,0,1:T(8,128)(2,1)} collective-permute-done((bf16[64,1,1280]{2,0,1:T(8,128)(2,1)S(1)}, bf16[64,1,1280]{2,0,1:T(8,128)(2,1)}, u32[]{:S(2)}, u32[]{:S(2)}) %collective-permute-start.1) | collective-permute-done | bytes 163872 | tf_op jit(solution)/shard_map/ppermute | solution.py:16
  24.4 7.1 %collective-permute-done.2 = bf16[64,1,1280]{2,0,1:T(8,128)(2,1)} collective-permute-done((bf16[64,1,1280]{2,0,1:T(8,128)(2,1)}, bf16[64,1,1280]{2,0,1:T(8,128)(2,1)}, u32[]{:S(2)}, u32[]{:S(2)}) %collective-permute-start.2) | collective-permute-done | bytes 163872 | tf_op jit(solution)/shard_map/ppermute | solution.py:16
  32.1 3.1 fusion.61
  36.8 6.6 %collective-permute-done.3 = bf16[64,1,1280]{2,0,1:T(8,128)(2,1)} collective-permute-done((bf16[64,1,1280]{2,0,1:T(8,128)(2,1)}, bf16[64,1,1280]{2,0,1:T(8,128)(2,1)}, u32[]{:S(2)}, u32[]{:S(2)}) %collective-permute-start.3) | collective-permute-done | bytes 163872 | tf_op jit(solution)/shard_map/ppermute | solution.py:16
  45.0 6.0 %collective-permute-done.4 = bf16[64,1,1280]{2,0,1:T(8,128)(2,1)S(1)} collective-permute-done((bf16[64,1,1280]{2,0,1:T(8,128)(2,1)}, bf16[64,1,1280]{2,0,1:T(8,128)(2,1)S(1)}, u32[]{:S(2)}, u32[]{:S(2)}) %collective-permute-start.4) | collective-permute-done | bytes 163872 | tf_op jit(solution)/shard_map/ppermute | solution.py:16
  51.0 9.9 %collective-permute-done.5 = bf16[64,1,1280]{2,0,1:T(8,128)(2,1)S(1)} collective-permute-done((bf16[64,1,1280]{2,0,1:T(8,128)(2,1)S(1)}, bf16[64,1,1280]{2,0,1:T(8,128)(2,1)S(1)}, u32[]{:S(2)}, u32[]{:S(2)}) %collective-permute-start.5) | collective-permute-done | bytes 163872 | tf_op jit(solution)/shard_map/ppermute | solution.py:16
  63.0 10.4 %collective-permute-done.6 = bf16[64,1,1280]{2,0,1:T(8,128)(2,1)S(1)} collective-permute-done((bf16[64,1,1280]{2,0,1:T(8,128)(2,1)S(1)}, bf16[64,1,1280]{2,0,1:T(8,128)(2,1)S(1)}, u32[]{:S(2)}, u32[]{:S(2)}) %collective-permute-start.6) | collective-permute-done | bytes 163872 | tf_op jit(solution)/shard_map/ppermute | solution.py:16
  74.1 12.2 %collective-permute-done.7 = bf16[64,1,1280]{2,0,1:T(8,128)(2,1)S(1)} collective-permute-done((bf16[64,1,1280]{2,0,1:T(8,128)(2,1)S(1)}, bf16[64,1,1280]{2,0,1:T(8,128)(2,1)S(1)}, u32[]{:S(2)}, u32[]{:S(2)}) %collective-permute-start.7) | collective-permute-done | bytes 163872 | tf_op jit(solution)/shard_map/ppermute | solution.py:16
  86.3 12.6 %collective-permute-done.8 = bf16[64,1,1280]{2,0,1:T(8,128)(2,1)S(1)} collective-permute-done((bf16[64,1,1280]{2,0,1:T(8,128)(2,1)S(1)}, bf16[64,1,1280]{2,0,1:T(8,128)(2,1)S(1)}, u32[]{:S(2)}, u32[]{:S(2)}) %collective-permute-start.8) | collective-permute-done | bytes 163872 | tf_op jit(solution)/shard_map/ppermute | solution.py:16
  99.5 6.9 %collective-permute-done.9 = bf16[64,1,1280]{2,0,1:T(8,128)(2,1)S(1)} collective-permute-done((bf16[64,1,1280]{2,0,1:T(8,128)(2,1)S(1)}, bf16[64,1,1280]{2,0,1:T(8,128)(2,1)S(1)}, u32[]{:S(2)}, u32[]{:S(2)}) %collective-permute-start.9) | collective-permute-done | bytes 163872 | tf_op jit(solution)/shard_map/ppermute | solution.py:16
  106.4 7.4 %collective-permute-done.10 = bf16[64,1,1280]{2,0,1:T(8,128)(2,1)S(1)} collective-permute-done((bf16[64,1,1280]{2,0,1:T(8,128)(2,1)S(1)}, bf16[64,1,1280]{2,0,1:T(8,128)(2,1)S(1)}, u32[]{:S(2)}, u32[]{:S(2)}) %collective-permute-start.10) | collective-permute-done | bytes 163872 | tf_op jit(solution)/shard_map/ppermute | solution.py:16
  115.2 6.2 %collective-permute-done.11 = bf16[64,1,1280]{2,0,1:T(8,128)(2,1)S(1)} collective-permute-done((bf16[64,1,1280]{2,0,1:T(8,128)(2,1)S(1)}, bf16[64,1,1280]{2,0,1:T(8,128)(2,1)S(1)}, u32[]{:S(2)}, u32[]{:S(2)}) %collective-permute-start.11) | collective-permute-done | bytes 163872 | tf_op jit(solution)/shard_map/ppermute | solution.py:16
  121.4 7.6 %collective-permute-done.12 = bf16[64,1,1280]{2,0,1:T(8,128)(2,1)} collective-permute-done((bf16[64,1,1280]{2,0,1:T(8,128)(2,1)S(1)}, bf16[64,1,1280]{2,0,1:T(8,128)(2,1)}, u32[]{:S(2)}, u32[]{:S(2)}) %collective-permute-start.12) | collective-permute-done | bytes 163872 | tf_op jit(solution)/shard_map/ppermute | solution.py:16
  131.0 13.0 %gather_fusion.6 = s32[1024]{0:T(1024)} fusion(s32[16,640]{1,0:T(8,128)S(1)} %gather_fusion, s32[1024]{0:T(1024)S(1)} %reshape.339), kind=kCustom, calls=%fused_computation.6 | custom fusion | bytes 16384 | tf_op jit(solution)/shard_map/jit(take_along_axis)/gather | solution.py:126
  195.6 11.3 %convolution_bitcast_fusion = f32[1,640,16,3,64]{1,4,3,2,0:T(8,128)} fusion(bf16[16,3,64,1280]{3,2,1,0:T(8,128)(2,1)} %bitcast.95, bf16[1,640,1280]{2,1,0:T(8,128)(2,1)} %param.13, f32[1280]{0:T(1024)S(1)} %copy-done.33, f32[640]{0:T(1024)S(1)} %copy-done.30, f32[640]{0:T(1024)S(1)} %copy-done.28), kind=kOutput, calls=%fused_computation.15 | convolution fusion | flops 5037260800 | bytes 17377280 | tf_op jit(solution)/shard_map/dot_general | solution.py:136
  206.9 15.1 %copy.40 = f32[1,640,16,3,64]{4,2,3,1,0:T(8,128)} copy(f32[1,640,16,3,64]{1,4,3,2,0:T(8,128)} %convolution_bitcast_fusion) | data formatting | bytes 15728640 | tf_op jit(solution)/shard_map/dot_general | solution.py:136
  222.0 3.5 %slice_bitcast_fusion = f32[1,640,16,64]{1,3,2,0:T(8,128)} fusion(f32[1,640,16,3,64]{1,4,3,2,0:T(8,128)} %convolution_bitcast_fusion), kind=kLoop, calls=%fused_computation.25 | loop fusion | bytes 5242880 | tf_op jit(solution)/shard_map/squeeze | solution.py:77
  225.6 7.0 %gather_fusion.2 = f32[64,16,64]{2,1,0:T(8,128)} fusion(f32[1,640,16,3,64]{4,2,3,1,0:T(8,128)} %copy.40, s32[64]{0:T(128)S(1)} %or_bitcast_fusion), kind=kCustom, calls=%fused_computation.2 | custom fusion | bytes 525056 | tf_op jit(solution)/shard_map/gather | solution.py:80
  236.1 2.6 fusion.27
  240.9 5.2 %fusion.16 = f32[1,64,1280]{2,1,0:T(8,128)} fusion(bf16[64,32,1280]{2,0,1:T(8,128)(2,1)} %constant_dynamic-update-slice_fusion, s32[]{:T(128)S(6)} %select_n.108, f32[16,64,640]{2,1,0:T(8,128)} %get-tuple-element.16, f32[16,64]{1,0:T(8,128)S(1)} %get-tuple-element.15, f32[1,640,16,3,64]{1,4,3,2,0:T(8,128)} %convolution_bitcast_fusion, ...), kind=kOutput, calls=%fused_computation.28 | convolution fusion | flops 253198336 | bytes 7049220 | tf_op jit(solution)/shard_map/cmhd,dhe->cme/dot_general | solution.py:95
  248.1 7.4 %all-to-all-start = ((f32[1,64,1280]{2,0,1:T(1,128)}), f32[1,64,1280]{2,0,1:T(1,128)}, u32[]{:S(2)}, u32[]{:S(2)}) async-start(f32[1,64,1280]{2,0,1:T(1,128)} %copy.45), calls=%async_computation | async-start | bytes 655360 | tf_op jit(solution)/shard_map/all_to_all | solution.py:144
  255.5 7.9 %all-to-all-done = f32[1,64,1280]{2,0,1:T(1,128)} async-done(((f32[1,64,1280]{2,0,1:T(1,128)}), f32[1,64,1280]{2,0,1:T(1,128)}, u32[]{:S(2)}, u32[]{:S(2)}) %all-to-all-start) | async-done | bytes 327712 | tf_op jit(solution)/shard_map/all_to_all | solution.py:144
  270.0 38.7 %all-gather = f32[16,16,4]{1,2,0:T(4,128)S(1)} all-gather(f32[1,16,4]{1,2,0:T(4,128)S(1)} %copy.46), channel_id=1, replica_groups=mesh['dp'=16,'mp'=16] {'dp'}, dimensions={0}, use_global_device_ids=true | all-gather | bytes 4352 | tf_op jit(solution)/shard_map/all_gather | solution.py:148
  (187 shorter events, 84.7 us)
Async XLA Ops:
  6.5 260.4 %copy-start = (bf16[1280,1280]{1,0:T(8,128)(2,1)S(1)}, bf16[1280,1280]{1,0:T(8,128)(2,1)}, u32[]{:S(2)}) copy-start(bf16[1280,1280]{1,0:T(8,128)(2,1)} %param.18) | copy-start | bytes 9830404
  6.5 123.7 %copy-start.2 = (s32[24,640]{1,0:T(8,128)S(1)}, s32[24,640]{1,0:T(8,128)}, u32[]{:S(2)}) copy-start(s32[24,640]{1,0:T(8,128)} %param.21) | copy-start | bytes 184324
  6.5 189.1 %all-gather.3.cloned.1.call-start = ((), (), s32[]{:S(2)}) async-start(), calls=%async_computation.1 | async-start | bytes 8355840 | tf_op jit(solution)/shard_map/all_gather | solution.py:133
  7.3 8.8 %collective-permute-start = (bf16[64,1,1280]{2,0,1:T(8,128)(2,1)}, bf16[64,1,1280]{2,0,1:T(8,128)(2,1)S(1)}, u32[]{:S(2)}, u32[]{:S(2)}) collective-permute-start(bf16[64,1,1280]{2,0,1:T(8,128)(2,1)} %param.16), channel_id=1, source_target_pairs={{0,1},{1,2},{2,3},{3,4},{4,5},{5,6},{6,7},{7,8},{8,9},{9,10},{10,1... | collective-permute-start | bytes 491528 | tf_op jit(solution)/shard_map/ppermute | solution.py:16
  16.0 114.9 %copy-start.4 = (bf16[64,1,1280]{2,0,1:T(8,128)(2,1)}, bf16[64,1,1280]{2,0,1:T(8,128)(2,1)S(1)}, u32[]{:S(2)}) copy-start(bf16[64,1,1280]{2,0,1:T(8,128)(2,1)S(1)} %collective-permute-done) | copy-start | bytes 491524
  16.0 7.6 %collective-permute-start.1 = (bf16[64,1,1280]{2,0,1:T(8,128)(2,1)S(1)}, bf16[64,1,1280]{2,0,1:T(8,128)(2,1)}, u32[]{:S(2)}, u32[]{:S(2)}) collective-permute-start(bf16[64,1,1280]{2,0,1:T(8,128)(2,1)S(1)} %collective-permute-done), channel_id=1, source_target_pairs={{0,1},{1,2},{2,3},{3,4},{4,5},{5,6},{6,7},{7,8},{8,9},{9,10},{10,1... | collective-permute-start | bytes 491528 | tf_op jit(solution)/shard_map/ppermute | solution.py:16
  23.6 7.9 %collective-permute-start.2 = (bf16[64,1,1280]{2,0,1:T(8,128)(2,1)}, bf16[64,1,1280]{2,0,1:T(8,128)(2,1)}, u32[]{:S(2)}, u32[]{:S(2)}) collective-permute-start(bf16[64,1,1280]{2,0,1:T(8,128)(2,1)} %collective-permute-done.1), channel_id=1, source_target_pairs={{0,1},{1,2},{2,3},{3,4},{4,5},{5,6},{6,7},{7,8},{8,9},{9,10},{10,1... | collective-permute-start | bytes 491528 | tf_op jit(solution)/shard_map/ppermute | solution.py:16
  31.5 11.8 %collective-permute-start.3 = (bf16[64,1,1280]{2,0,1:T(8,128)(2,1)}, bf16[64,1,1280]{2,0,1:T(8,128)(2,1)}, u32[]{:S(2)}, u32[]{:S(2)}) collective-permute-start(bf16[64,1,1280]{2,0,1:T(8,128)(2,1)} %collective-permute-done.2), channel_id=1, source_target_pairs={{0,1},{1,2},{2,3},{3,4},{4,5},{5,6},{6,7},{7,8},{8,9},{9,10},{10,1... | collective-permute-start | bytes 491528 | tf_op jit(solution)/shard_map/ppermute | solution.py:16
  43.3 7.7 %collective-permute-start.4 = (bf16[64,1,1280]{2,0,1:T(8,128)(2,1)}, bf16[64,1,1280]{2,0,1:T(8,128)(2,1)S(1)}, u32[]{:S(2)}, u32[]{:S(2)}) collective-permute-start(bf16[64,1,1280]{2,0,1:T(8,128)(2,1)} %collective-permute-done.3), channel_id=1, source_target_pairs={{0,1},{1,2},{2,3},{3,4},{4,5},{5,6},{6,7},{7,8},{8,9},{9,10},{10,1... | collective-permute-start | bytes 491528 | tf_op jit(solution)/shard_map/ppermute | solution.py:16
  51.0 78.0 %copy-start.6 = (bf16[64,1,1280]{2,0,1:T(8,128)(2,1)}, bf16[64,1,1280]{2,0,1:T(8,128)(2,1)S(1)}, u32[]{:S(2)}) copy-start(bf16[64,1,1280]{2,0,1:T(8,128)(2,1)S(1)} %collective-permute-done.4) | copy-start | bytes 491524
  51.0 9.9 %collective-permute-start.5 = (bf16[64,1,1280]{2,0,1:T(8,128)(2,1)S(1)}, bf16[64,1,1280]{2,0,1:T(8,128)(2,1)S(1)}, u32[]{:S(2)}, u32[]{:S(2)}) collective-permute-start(bf16[64,1,1280]{2,0,1:T(8,128)(2,1)S(1)} %collective-permute-done.4), channel_id=1, source_target_pairs={{0,1},{1,2},{2,3},{3,4},{4,5},{5,6},{6,7},{7,8},{8,9},{9,10},{10,1... | collective-permute-start | bytes 491528 | tf_op jit(solution)/shard_map/ppermute | solution.py:16
  51.0 70.3 %copy-start.27 = (f32[640]{0:T(1024)}, f32[640]{0:T(1024)S(1)}, u32[]{:S(2)}) copy-start(f32[640]{0:T(1024)S(1)} %broadcast_multiply_fusion.1) | copy-start | bytes 7684
  61.0 68.0 %copy-start.8 = (bf16[64,1,1280]{2,0,1:T(8,128)(2,1)}, bf16[64,1,1280]{2,0,1:T(8,128)(2,1)S(1)}, u32[]{:S(2)}) copy-start(bf16[64,1,1280]{2,0,1:T(8,128)(2,1)S(1)} %collective-permute-done.5) | copy-start | bytes 491524
  61.0 12.5 %collective-permute-start.6 = (bf16[64,1,1280]{2,0,1:T(8,128)(2,1)S(1)}, bf16[64,1,1280]{2,0,1:T(8,128)(2,1)S(1)}, u32[]{:S(2)}, u32[]{:S(2)}) collective-permute-start(bf16[64,1,1280]{2,0,1:T(8,128)(2,1)S(1)} %collective-permute-done.5), channel_id=1, source_target_pairs={{0,1},{1,2},{2,3},{3,4},{4,5},{5,6},{6,7},{7,8},{8,9},{9,10},{10,1... | collective-permute-start | bytes 491528 | tf_op jit(solution)/shard_map/ppermute | solution.py:16
  73.4 55.5 %copy-start.10 = (bf16[64,1,1280]{2,0,1:T(8,128)(2,1)}, bf16[64,1,1280]{2,0,1:T(8,128)(2,1)S(1)}, u32[]{:S(2)}) copy-start(bf16[64,1,1280]{2,0,1:T(8,128)(2,1)S(1)} %collective-permute-done.6) | copy-start | bytes 491524
  73.4 12.9 %collective-permute-start.7 = (bf16[64,1,1280]{2,0,1:T(8,128)(2,1)S(1)}, bf16[64,1,1280]{2,0,1:T(8,128)(2,1)S(1)}, u32[]{:S(2)}, u32[]{:S(2)}) collective-permute-start(bf16[64,1,1280]{2,0,1:T(8,128)(2,1)S(1)} %collective-permute-done.6), channel_id=1, source_target_pairs={{0,1},{1,2},{2,3},{3,4},{4,5},{5,6},{6,7},{7,8},{8,9},{9,10},{10,1... | collective-permute-start | bytes 491528 | tf_op jit(solution)/shard_map/ppermute | solution.py:16
  86.3 12.6 %collective-permute-start.8 = (bf16[64,1,1280]{2,0,1:T(8,128)(2,1)S(1)}, bf16[64,1,1280]{2,0,1:T(8,128)(2,1)S(1)}, u32[]{:S(2)}, u32[]{:S(2)}) collective-permute-start(bf16[64,1,1280]{2,0,1:T(8,128)(2,1)S(1)} %collective-permute-done.7), channel_id=1, source_target_pairs={{0,1},{1,2},{2,3},{3,4},{4,5},{5,6},{6,7},{7,8},{8,9},{9,10},{10,1... | collective-permute-start | bytes 491528 | tf_op jit(solution)/shard_map/ppermute | solution.py:16
  98.9 7.5 %collective-permute-start.9 = (bf16[64,1,1280]{2,0,1:T(8,128)(2,1)S(1)}, bf16[64,1,1280]{2,0,1:T(8,128)(2,1)S(1)}, u32[]{:S(2)}, u32[]{:S(2)}) collective-permute-start(bf16[64,1,1280]{2,0,1:T(8,128)(2,1)S(1)} %collective-permute-done.8), channel_id=1, source_target_pairs={{0,1},{1,2},{2,3},{3,4},{4,5},{5,6},{6,7},{7,8},{8,9},{9,10},{10,1... | collective-permute-start | bytes 491528 | tf_op jit(solution)/shard_map/ppermute | solution.py:16
  106.4 7.5 %collective-permute-start.10 = (bf16[64,1,1280]{2,0,1:T(8,128)(2,1)S(1)}, bf16[64,1,1280]{2,0,1:T(8,128)(2,1)S(1)}, u32[]{:S(2)}, u32[]{:S(2)}) collective-permute-start(bf16[64,1,1280]{2,0,1:T(8,128)(2,1)S(1)} %collective-permute-done.9), channel_id=1, source_target_pairs={{0,1},{1,2},{2,3},{3,4},{4,5},{5,6},{6,7},{7,8},{8,9},{9,10},{10,1... | collective-permute-start | bytes 491528 | tf_op jit(solution)/shard_map/ppermute | solution.py:16
  113.9 7.5 %collective-permute-start.11 = (bf16[64,1,1280]{2,0,1:T(8,128)(2,1)S(1)}, bf16[64,1,1280]{2,0,1:T(8,128)(2,1)S(1)}, u32[]{:S(2)}, u32[]{:S(2)}) collective-permute-start(bf16[64,1,1280]{2,0,1:T(8,128)(2,1)S(1)} %collective-permute-done.10), channel_id=1, source_target_pairs={{0,1},{1,2},{2,3},{3,4},{4,5},{5,6},{6,7},{7,8},{8,9},{9,10},{10,1... | collective-permute-start | bytes 491528 | tf_op jit(solution)/shard_map/ppermute | solution.py:16
  121.4 7.6 %collective-permute-start.12 = (bf16[64,1,1280]{2,0,1:T(8,128)(2,1)S(1)}, bf16[64,1,1280]{2,0,1:T(8,128)(2,1)}, u32[]{:S(2)}, u32[]{:S(2)}) collective-permute-start(bf16[64,1,1280]{2,0,1:T(8,128)(2,1)S(1)} %collective-permute-done.11), channel_id=1, source_target_pairs={{0,1},{1,2},{2,3},{3,4},{4,5},{5,6},{6,7},{7,8},{8,9},{9,10},{10,1... | collective-permute-start | bytes 491528 | tf_op jit(solution)/shard_map/ppermute | solution.py:16
  129.0 16.6 %collective-permute-start.13 = (bf16[64,1,1280]{2,0,1:T(8,128)(2,1)}, bf16[64,1,1280]{2,0,1:T(8,128)(2,1)}, u32[]{:S(2)}, u32[]{:S(2)}) collective-permute-start(bf16[64,1,1280]{2,0,1:T(8,128)(2,1)} %collective-permute-done.12), channel_id=1, source_target_pairs={{0,1},{1,2},{2,3},{3,4},{4,5},{5,6},{6,7},{7,8},{8,9},{9,10},{10,1... | collective-permute-start | bytes 491528 | tf_op jit(solution)/shard_map/ppermute | solution.py:16
  145.5 9.1 %collective-permute-start.14 = (bf16[64,1,1280]{2,0,1:T(8,128)(2,1)}, bf16[64,1,1280]{2,0,1:T(8,128)(2,1)}, u32[]{:S(2)}, u32[]{:S(2)}) collective-permute-start(bf16[64,1,1280]{2,0,1:T(8,128)(2,1)} %collective-permute-done.13), channel_id=1, source_target_pairs={{0,1},{1,2},{2,3},{3,4},{4,5},{5,6},{6,7},{7,8},{8,9},{9,10},{10,1... | collective-permute-start | bytes 491528 | tf_op jit(solution)/shard_map/ppermute | solution.py:16
  248.1 15.3 %all-to-all-start = ((f32[1,64,1280]{2,0,1:T(1,128)}), f32[1,64,1280]{2,0,1:T(1,128)}, u32[]{:S(2)}, u32[]{:S(2)}) async-start(f32[1,64,1280]{2,0,1:T(1,128)} %copy.45), calls=%async_computation | async-start | bytes 655360 | tf_op jit(solution)/shard_map/all_to_all | solution.py:144
  (29 other events, 681.6 us)
Sparse Core Ops, SparseCore 0:
  9.8 92.8 all-gather.2
